TPU v7x, 128 devices: a whole 4x4x4 slice. The times are simulated.
128 devices in a mesh: fsdp: 32 (over z, y, core), slide: 4 (over x).
Axes of the slice: x: 4, y: 4, z: 4, core: 2. Of those that a mesh axis runs over, the one named last changes fastest.
Arguments:
- tiles: bfloat16 [65536, 1536], P(('slide', 'fsdp')), parts along dimension 0, may hold values from -6 to 6
- tile_cell: int32 [65536], P('slide'), parts along dimension 0, may hold values from 0 to 16383, as said below
- tissue: int32 [256, 256], P('slide'), parts along dimension 0, may hold values 0 or 1
- norm_gain: float32 [2, 1536], replicated, may hold values from 0.5 to 1.5
- qk_gain: float32 [2, 2, 64], replicated, may hold values from 0.5 to 4
- row_qkv: bfloat16 [1536, 4608], P(None, 'fsdp'), may hold values from -0.15625 to 0.15625
- row_out: bfloat16 [1536, 1536], P(None, 'fsdp'), may hold values from -0.15625 to 0.15625
- col_qkv: bfloat16 [1536, 4608], P(None, 'fsdp'), may hold values from -0.15625 to 0.15625
- col_out: bfloat16 [1536, 1536], P(None, 'fsdp'), may hold values from -0.15625 to 0.15625
Outputs:
- encoded: bfloat16 [256, 256, 1536], P('slide', 'fsdp'), parts along dimension 0
There are 4 independent parts, one for each index of `slide`. A program takes and returns all parts, laid end to end along the dimension named above; an argument that names none is the same for every part. Nothing has to cross between parts.
Inputs may be any that keep to these rules, and one draw needn't show every extreme that they name: Slots d * 512 + b * 16 up to d * 512 + (b + 1) * 16 - 1 hold tiles of grid rows b * 2 to (b + 1) * 2 - 1; tile_cell names every grid cell exactly once.
All inputs are finite; a program needn't handle non-finite values.
Results may differ from a plain program's by a relative error of at most 0.02.
The roundings to bfloat16 on the way count: a program that leaves them out, or rounds other values in their place, can miss the bound.
Values may be sent and summed in bfloat16 or wider, within the bound.
No kernel may reach another device: no remote copies, remote signals or barrier semaphores. Data moves between devices by JAX's collectives and lax.ppermute only.
A program may use at most 256 MiB of HBM per device.

v0:
```python
import jax
import jax.numpy as jnp
from jax import lax
from jax.sharding import PartitionSpec as P

HEADS = 24
EPS = 1e-06


def rms_norm(grid, gain):
    values = grid.astype(jnp.float32)
    scale = lax.rsqrt(jnp.mean(values * values, axis=-1, keepdims=True) + EPS)
    return (values * scale * gain).astype(jnp.bfloat16)


def head_norm(values, gain):
    scale = lax.rsqrt(jnp.mean(values * values, axis=-1, keepdims=True) + EPS)
    return values * scale * gain


def rotate(values, rows_pos, cols_pos):
    quarter = values.shape[-1] // 4
    freq = 10000.0 ** (-jnp.arange(quarter).astype(jnp.float32) / quarter)

    def turn(part, position):
        angle = position.astype(jnp.float32)[..., None, None] * freq
        cosine = jnp.cos(angle)
        sine = jnp.sin(angle)
        first = part[..., :quarter]
        second = part[..., quarter:]
        return jnp.concatenate(
            [first * cosine - second * sine, first * sine + second * cosine], axis=-1
        )

    half = 2 * quarter
    return jnp.concatenate(
        [turn(values[..., :half], rows_pos), turn(values[..., half:], cols_pos)], axis=-1
    )


def attend(qkv, gains, rows_pos, cols_pos, keys_live, column, heads):
    width = qkv.shape[-1] // 3
    size = width // heads
    shape = qkv.shape[:-1] + (heads, size)
    query = qkv[..., :width].reshape(shape).astype(jnp.float32)
    key = qkv[..., width : 2 * width].reshape(shape).astype(jnp.float32)
    value = qkv[..., 2 * width :].reshape(shape)
    query = rotate(head_norm(query, gains[0]), rows_pos, cols_pos).astype(jnp.bfloat16)
    key = rotate(head_norm(key, gains[1]), rows_pos, cols_pos).astype(jnp.bfloat16)
    if column:
        score_form = "lbhd,mbhd->bhlm"
        mix_form = "bhlm,mbhd->lbhd"
        live = keys_live.T
    else:
        score_form = "blhd,bmhd->bhlm"
        mix_form = "bhlm,bmhd->blhd"
        live = keys_live
    scores = jnp.einsum(score_form, query, key, preferred_element_type=jnp.float32) * size ** (-0.5)
    length = scores.shape[-1]
    diagonal = jnp.arange(length)[:, None] == jnp.arange(length)[None, :]
    allow = (live[:, None, None, :] > 0) | diagonal[None, None]
    scores = jnp.where(allow, scores, -1e30)
    top = jnp.max(scores, axis=-1, keepdims=True)
    weights = jnp.exp(scores - top)
    total = jnp.sum(weights, axis=-1)
    mixed = jnp.einsum(
        mix_form, weights.astype(jnp.bfloat16), value, preferred_element_type=jnp.float32
    )
    if column:
        total = total.transpose(2, 0, 1)
    else:
        total = total.transpose(0, 2, 1)
    return (mixed / total[..., None]).reshape(qkv.shape[:-1] + (width,)).astype(jnp.bfloat16)


def project_qkv(normed, weight):

    def multiply(piece, start):
        return jnp.dot(normed, piece, preferred_element_type=jnp.float32)

    return multiply(lax.all_gather(weight, "fsdp", axis=1, tiled=True), jnp.int32(0)).astype(
        jnp.bfloat16
    )


def project_out(mixed, weight):

    def multiply(piece, start):
        return jnp.dot(mixed, piece, preferred_element_type=jnp.float32)

    return multiply(lax.all_gather(weight, "fsdp", axis=1, tiled=True), jnp.int32(0))


def on_device(tiles, tile_cell, tissue, norm_gain, qk_gain, row_qkv, row_out, col_qkv, col_out):
    count = lax.axis_size("fsdp")
    index = lax.axis_index("fsdp")
    width = tiles.shape[1]
    tok_dev = tiles.shape[0]
    slots = tok_dev // count
    grid_rows = tissue.shape[0]
    columns = tissue.shape[1]
    rows_dev = grid_rows // count
    cols_dev = columns // count
    arrived = lax.all_to_all(
        tiles.reshape(count, slots, width), "fsdp", split_axis=0, concat_axis=0, tiled=True
    )
    table_cell = lax.dynamic_index_in_dim(
        tile_cell.reshape(count, count, slots), index, 1, keepdims=False
    )
    row_base = index * rows_dev
    local_cells = (table_cell - row_base * columns).reshape(-1)
    grid = (
        jnp.zeros((tok_dev, width), jnp.bfloat16)
        .at[local_cells]
        .set(arrived.reshape(tok_dev, width))
    )
    rows_pos = row_base + lax.broadcasted_iota(jnp.int32, (rows_dev, columns), 0)
    cols_pos = lax.broadcasted_iota(jnp.int32, (rows_dev, columns), 1)
    live_rows = lax.dynamic_slice_in_dim(tissue, row_base, rows_dev, 0)
    qkv = project_qkv(rms_norm(grid, norm_gain[0]), row_qkv).reshape(rows_dev, columns, 3 * width)
    mixed = attend(qkv, qk_gain[0], rows_pos, cols_pos, live_rows, False, HEADS)
    hidden = grid.astype(jnp.float32) + project_out(mixed.reshape(tok_dev, width), row_out)
    hidden = hidden.astype(jnp.bfloat16).reshape(rows_dev, columns, width)
    turned = lax.all_to_all(hidden, "fsdp", split_axis=1, concat_axis=0, tiled=True)
    col_base = index * cols_dev
    rows_pos_col = lax.broadcasted_iota(jnp.int32, (grid_rows, cols_dev), 0)
    cols_pos_col = col_base + lax.broadcasted_iota(jnp.int32, (grid_rows, cols_dev), 1)
    live_cols = lax.dynamic_slice_in_dim(tissue, col_base, cols_dev, 1)
    flat = turned.reshape(grid_rows * cols_dev, width)
    qkv_col = project_qkv(rms_norm(flat, norm_gain[1]), col_qkv).reshape(
        grid_rows, cols_dev, 3 * width
    )
    mixed_col = attend(qkv_col, qk_gain[1], rows_pos_col, cols_pos_col, live_cols, True, HEADS)
    result = flat.astype(jnp.float32) + project_out(
        mixed_col.reshape(grid_rows * cols_dev, width), col_out
    )
    return result.astype(jnp.bfloat16).reshape(grid_rows, cols_dev, width)


def solution(mesh):
    return jax.shard_map(
        on_device,
        mesh=mesh,
        in_specs=(
            P(("slide", "fsdp"), None),
            P("slide"),
            P("slide", None),
            P(),
            P(),
            P(None, "fsdp"),
            P(None, "fsdp"),
            P(None, "fsdp"),
            P(None, "fsdp"),
        ),
        out_specs=P("slide", "fsdp", None),
        check_vma=False,
    )
```

profile of v0, /device:TPU:1, one launch (start us, length us, event | category | flops | bytes accessed | tf_op | source)
XLA Modules:
  0.0 325.4 jit_solution(16817885451585981338)
XLA Ops:
  8.8 9.6 %all-to-all-start = ((bf16[32,16,1536]{2,1,0:T(8,128)(2,1)}), bf16[32,16,1536]{2,1,0:T(8,128)(2,1)S(1)}, u32[]{:S(2)}, u32[]{:S(2)}) async-start(bf16[32,16,1536]{2,1,0:T(8,128)(2,1)} %bitcast.73), calls=%async_computation | async-start | bytes 3145728 | tf_op jit(solution)/shard_map/all_to_all | solution.py:104
  19.3 27.7 %all-to-all-done = bf16[32,16,1536]{2,1,0:T(8,128)(2,1)S(1)} async-done(((bf16[32,16,1536]{2,1,0:T(8,128)(2,1)}), bf16[32,16,1536]{2,1,0:T(8,128)(2,1)S(1)}, u32[]{:S(2)}, u32[]{:S(2)}) %all-to-all-start) | async-done | bytes 1572896 | tf_op jit(solution)/shard_map/all_to_all | solution.py:104
  46.9 3.4 %scatter_custom_fusion = bf16[512,1536]{1,0:T(8,128)(2,1)S(1)} fusion(s32[512]{0:T(512)S(1)} %bitcast.80, bf16[512,1536]{1,0:T(8,128)(2,1)S(1)} %bitcast.74, bf16[]{:T(256)} %constant.19.clone.1), kind=kCustom, calls=%fused_computation.104 | custom fusion | bytes 1572866 | tf_op jit(solution)/shard_map/scatter | solution.py:115
  50.8 38.5 %all-gather.5.cloned.1.call-done = bf16[1536,4608]{0,1:T(8,128)(2,1)} async-done(((bf16[1536,144]{0,1:T(8,128)(2,1)}), bf16[1536,4608]{0,1:T(8,128)(2,1)}) %all-gather.5.cloned.1.call-update) | async-done | bytes 14155792 | tf_op jit(solution)/shard_map/all_gather | solution.py:81
  89.3 11.1 %convolution_convert_fusion.1 = bf16[512,4608]{1,0:T(8,128)(2,1)S(1)} fusion(bf16[1536,4608]{0,1:T(8,128)(2,1)} %all-gather.5.cloned.1.call-done, bf16[512,1536]{1,0:T(8,128)(2,1)S(1)} %scatter_custom_fusion, f32[1536]{0:T(1024)S(1)} %get-tuple-element.6, f32[512]{0:T(512)S(1)} %add_rsqrt_fusion.5), kind=kOutput, calls=%fused_computation.7 | convolution fusion | flops 7253262336 | bytes 20455424 | tf_op jit(solution)/shard_map/dot_general | solution.py:79
  121.7 3.5 %fusion.38 = bf16[2,256,24,64]{1,3,2,0:T(8,128)(2,1)S(1)} fusion(bf16[2,256,24,64]{1,3,2,0:T(8,128)(2,1)S(1)} %bitcast.75, f32[2,24,256,256]{2,3,1,0:T(8,128)S(1)} %get-tuple-element.54, f32[2,24,256]{2,1,0:T(8,128)S(1)} %get-tuple-element.53, pred[2,256,256]{1,2,0:T(8,128)(4,1)S(1)} %broadcast_or_fusion, f32[2,256,24]{1,2,0:T(8,128)S(1)} %bitcast.79), kind=kOutput, calls=%fused_computation.62 | convolution fusion | flops 416808960 | bytes 15958016 | tf_op jit(solution)/shard_map/bhlm,bmhd->blhd/dot_general | solution.py:66
  127.1 10.6 %all-gather.7.cloned.1.call-done = bf16[1536,1536]{0,1:T(8,128)(2,1)} async-done(((bf16[1536,48]{0,1:T(8,128)(2,1)}), bf16[1536,1536]{0,1:T(8,128)(2,1)}) %all-gather.7.cloned.1.call-update) | async-done | bytes 4718608 | tf_op jit(solution)/shard_map/all_gather | solution.py:91
  137.8 5.0 %fusion.44 = bf16[512,1536]{1,0:T(8,128)(2,1)S(1)} fusion(bf16[512,1536]{0,1:T(8,128)(2,1)S(1)} %bitcast.76, bf16[1536,1536]{0,1:T(8,128)(2,1)} %all-gather.7.cloned.1.call-done, bf16[512,1536]{1,0:T(8,128)(2,1)S(1)} %copy-done.5), kind=kOutput, calls=%fused_computation.73 | convolution fusion | flops 2418278400 | bytes 9437184 | tf_op jit(solution)/shard_map/dot_general | solution.py:89
  145.5 5.3 %all-to-all-start.1 = ((bf16[2,256,1536]{2,0,1:T(2,128)(2,1)}), bf16[2,256,1536]{2,0,1:T(2,128)(2,1)S(1)}, u32[]{:S(2)}, u32[]{:S(2)}) async-start(bf16[2,256,1536]{2,0,1:T(2,128)(2,1)} %copy.69), calls=%async_computation.1 | async-start | bytes 3145728 | tf_op jit(solution)/shard_map/all_to_all | solution.py:124
  153.4 25.1 %all-to-all-done.1 = bf16[2,256,1536]{2,0,1:T(2,128)(2,1)S(1)} async-done(((bf16[2,256,1536]{2,0,1:T(2,128)(2,1)}), bf16[2,256,1536]{2,0,1:T(2,128)(2,1)S(1)}, u32[]{:S(2)}, u32[]{:S(2)}) %all-to-all-start.1) | async-done | bytes 1572896 | tf_op jit(solution)/shard_map/all_to_all | solution.py:124
  185.0 34.7 %all-gather.9.cloned.1.call-done = bf16[1536,4608]{0,1:T(8,128)(2,1)} async-done(((bf16[1536,144]{0,1:T(8,128)(2,1)}), bf16[1536,4608]{0,1:T(8,128)(2,1)}) %all-gather.9.cloned.1.call-update) | async-done | bytes 14155792 | tf_op jit(solution)/shard_map/all_gather | solution.py:81
  219.6 10.7 %fusion.3 = bf16[64,8,4608]{2,1,0:T(8,128)(2,1)S(1)} fusion(bf16[512,1536]{1,0:T(8,128)(2,1)S(1)} %fusion.37, bf16[1536,4608]{0,1:T(8,128)(2,1)} %all-gather.9.cloned.1.call-done), kind=kOutput, calls=%fused_computation.8 | convolution fusion | flops 7250116608 | bytes 20447232 | tf_op jit(solution)/shard_map/dot_general | solution.py:79
  230.4 3.2 fusion.77
  233.6 5.5 %reshape.257 = f32[64,8,24,64]{3,2,1,0:T(8,128)} reshape(f32[64,8,1536]{2,1,0:T(8,128)} %get-tuple-element.20) | data formatting | bytes 6291456 | tf_op jit(solution)/shard_map/convert_element_type | solution.py:46
  239.1 5.2 %multiply_reduce_fusion = f32[64,8,24]{2,1,0:T(8,128)} fusion(f32[64,8,24,64]{3,2,1,0:T(8,128)} %reshape.257), kind=kLoop, calls=%fused_computation.22 | loop fusion | flops 1560576 | bytes 3194880 | tf_op jit(solution)/shard_map/reduce_sum | solution.py:17
  246.0 3.5 %reshape.256 = f32[64,8,24,64]{3,2,1,0:T(8,128)} reshape(f32[64,8,1536]{2,1,0:T(8,128)S(1)} %get-tuple-element.21) | data formatting | bytes 6291456 | tf_op jit(solution)/shard_map/convert_element_type | solution.py:45
  249.5 5.0 %multiply_reduce_fusion.1 = f32[64,8,24]{2,1,0:T(8,128)S(1)} fusion(f32[64,8,24,64]{3,2,1,0:T(8,128)} %reshape.256), kind=kLoop, calls=%fused_computation.27 | loop fusion | flops 1560576 | bytes 3194880 | tf_op jit(solution)/shard_map/reduce_sum | solution.py:17
  258.0 9.4 %fusion.7 = (f32[64,8,24,64]{3,0,2,1:T(8,128)S(1)}, f32[64,8,24,64]{3,0,2,1:T(8,128)S(1)}) fusion(f32[64,8,24,64]{3,2,1,0:T(8,128)} %reshape.257, f32[64]{0:T(128)S(1)} %get-tuple-element.37, f32[64,8,24]{0,2,1:T(8,128)S(1)} %add_rsqrt_fusion.1, f32[64]{0:T(128)S(1)} %get-tuple-element.40, f32[64,8,24]{0,2,1:T(8,128)S(1)} %add_rsqrt_fusion.2, ...), kind=kLoop, calls=%fused_computation.13 | loop fusion | flops 3145728 | bytes 12681728 | tf_op jit(solution)/shard_map/mul | solution.py:18
  267.4 7.9 %subtract_convert_fusion.3 = (bf16[64,8,24,16]{3,0,2,1:T(8,128)(2,1)}, bf16[64,8,24,16]{3,0,2,1:T(8,128)(2,1)}, bf16[64,8,24,16]{3,0,2,1:T(8,128)(2,1)}, bf16[64,8,24,16]{3,0,2,1:T(8,128)(2,1)}) fusion(f32[64,8,24,64]{3,0,2,1:T(8,128)S(1)} %get-tuple-element.58, f32[64,8,16]{2,0,1:T(8,128)S(1)} %copy-done.8, f32[64,8,16]{2,0,1:T(8,128)S(1)} %get-tuple-element.43, ...), kind=kLoop, calls=%fused_computation.26 | loop fusion | flops 3145728 | bytes 4849664 | tf_op jit(solution)/shard_map/convert.11
  275.4 7.8 %subtract_convert_fusion.1 = (bf16[64,8,24,16]{3,0,2,1:T(8,128)(2,1)}, bf16[64,8,24,16]{3,0,2,1:T(8,128)(2,1)}, bf16[64,8,24,16]{3,0,2,1:T(8,128)(2,1)}, bf16[64,8,24,16]{3,0,2,1:T(8,128)(2,1)}) fusion(f32[64,8,24,64]{3,0,2,1:T(8,128)S(1)} %get-tuple-element.57, f32[64,8,16]{2,0,1:T(8,128)S(1)} %copy-done.8, f32[64,8,16]{2,0,1:T(8,128)S(1)} %get-tuple-element.43, ...), kind=kLoop, calls=%fused_computation.21 | loop fusion | flops 3145728 | bytes 4849664 | tf_op jit(solution)/shard_map/convert.7
  283.1 12.9 %fusion.13 = (f32[8,24,64]{2,1,0:T(8,128)S(1)}, f32[8,24,64,64]{2,3,1,0:T(8,128)S(1)}) fusion(pred[8,64,64]{1,2,0:T(8,128)(4,1)S(1)} %broadcast_or_fusion.1, bf16[64,8,24,16]{3,0,2,1:T(8,128)(2,1)} %get-tuple-element.15, bf16[64,8,24,16]{3,0,2,1:T(8,128)(2,1)} %get-tuple-element.16, bf16[64,8,24,16]{3,0,2,1:T(8,128)(2,1)} %get-tuple-element.8, ...), kind=kOutput, calls=%fused_computation.32 | convolution fusion | flops 115593216 | bytes 6373376 | tf_op jit(solution)/shard_map/lbhd,mbhd->bhlm/dot_general | solution.py:58
  301.3 5.3 %copy.80 = bf16[64,8,24,64]{3,2,1,0:T(8,128)(2,1)} copy(bf16[64,8,24,64]{0,3,2,1:T(8,128)(2,1)} %fusion.6) | data formatting | bytes 3145728 | tf_op jit(solution)/shard_map/convert_element_type | solution.py:73
  306.6 5.5 %convert_element_type.211 = bf16[512,1536]{1,0:T(8,128)(2,1)} reshape(bf16[64,8,24,64]{3,2,1,0:T(8,128)(2,1)} %copy.80) | data formatting | bytes 3145728 | tf_op jit(solution)/shard_map/convert_element_type | solution.py:73
  312.0 6.6 %fusion.45 = bf16[64,8,1536]{2,1,0:T(8,128)(2,1)} fusion(f32[512,1536]{1,0:T(8,128)S(1)} %bitcast.69, bf16[512,1536]{1,0:T(8,128)(2,1)} %convert_element_type.211, bf16[1536,1536]{0,1:T(8,128)(2,1)} %all-gather.11.cloned.1.call-done), kind=kOutput, calls=%fused_computation.74 | convolution fusion | flops 2417491968 | bytes 11010048 | tf_op jit(solution)/shard_map/dot_general | solution.py:89
  (95 shorter events, 48.5 us)
Async XLA Ops:
  6.5 11.9 %copy-start.13 = (s32[16384]{0:T(1024)S(1)}, s32[16384]{0:T(1024)}, u32[]{:S(2)}) copy-start(s32[16384]{0:T(1024)} %param.10) | copy-start | bytes 196612
  6.5 12.2 %copy-start.14 = (s32[64,256]{1,0:T(8,128)S(1)}, s32[64,256]{1,0:T(8,128)}, u32[]{:S(2)}) copy-start(s32[64,256]{1,0:T(8,128)} %param.11) | copy-start | bytes 196612
  6.5 12.3 %copy-start.15 = (f32[2,1536]{1,0:T(2,128)S(1)}, f32[2,1536]{1,0:T(2,128)}, u32[]{:S(2)}) copy-start(f32[2,1536]{1,0:T(2,128)} %param.12) | copy-start | bytes 36868
  6.5 12.3 %copy-start.16 = (f32[2,2,64]{2,1,0:T(2,128)S(1)}, f32[2,2,64]{2,1,0:T(2,128)}, u32[]{:S(2)}) copy-start(f32[2,2,64]{2,1,0:T(2,128)} %param.13) | copy-start | bytes 3076
  6.5 82.7 %all-gather.5.cloned.1.call-start = ((), (), s32[]{:S(2)}) async-start(), calls=%async_computation.2 | async-start | bytes 14598144 | tf_op jit(solution)/shard_map/all_gather | solution.py:81
  7.3 130.5 %all-gather.7.cloned.1.call-start = ((), (), s32[]{:S(2)}) async-start(), calls=%async_computation.3 | async-start | bytes 4866048 | tf_op jit(solution)/shard_map/all_gather | solution.py:91
  8.0 211.6 %all-gather.9.cloned.1.call-start = ((), (), s32[]{:S(2)}) async-start(), calls=%async_computation.4 | async-start | bytes 14598144 | tf_op jit(solution)/shard_map/all_gather | solution.py:81
  8.8 38.2 %all-to-all-start = ((bf16[32,16,1536]{2,1,0:T(8,128)(2,1)}), bf16[32,16,1536]{2,1,0:T(8,128)(2,1)S(1)}, u32[]{:S(2)}, u32[]{:S(2)}) async-start(bf16[32,16,1536]{2,1,0:T(8,128)(2,1)} %bitcast.73), calls=%async_computation | async-start | bytes 3145728 | tf_op jit(solution)/shard_map/all_to_all | solution.py:104
  50.4 50.0 %copy-start.4 = (bf16[512,1536]{1,0:T(8,128)(2,1)}, bf16[512,1536]{1,0:T(8,128)(2,1)S(1)}, u32[]{:S(2)}) copy-start(bf16[512,1536]{1,0:T(8,128)(2,1)S(1)} %scatter_custom_fusion) | copy-start | bytes 4718596
  110.9 2.9 copy-start
  118.5 3.1 copy-start.11
  125.1 12.6 %copy-start.5 = (bf16[512,1536]{1,0:T(8,128)(2,1)S(1)}, bf16[512,1536]{1,0:T(8,128)(2,1)}, u32[]{:S(2)}) copy-start(bf16[512,1536]{1,0:T(8,128)(2,1)} %copy-done.4) | copy-start | bytes 4718596
  145.5 33.0 %all-to-all-start.1 = ((bf16[2,256,1536]{2,0,1:T(2,128)(2,1)}), bf16[2,256,1536]{2,0,1:T(2,128)(2,1)S(1)}, u32[]{:S(2)}, u32[]{:S(2)}) async-start(bf16[2,256,1536]{2,0,1:T(2,128)(2,1)} %copy.69), calls=%async_computation.1 | async-start | bytes 3145728 | tf_op jit(solution)/shard_map/all_to_all | solution.py:124
  150.9 161.2 %all-gather.11.cloned.1.call-start = ((), (), s32[]{:S(2)}) async-start(), calls=%async_computation.5 | async-start | bytes 4866048 | tf_op jit(solution)/shard_map/all_gather | solution.py:91
  249.5 5.1 %copy-start.6 = (bf16[64,8,1536]{2,1,0:T(8,128)(2,1)S(1)}, bf16[64,8,1536]{2,1,0:T(8,128)(2,1)}, u32[]{:S(2)}) copy-start(bf16[64,8,1536]{2,1,0:T(8,128)(2,1)} %get-tuple-element.19) | copy-start | bytes 4718596
  254.5 3.4 %copy-start.12 = (f32[64,8,24]{0,2,1:T(8,128)S(1)}, f32[64,8,24]{0,2,1:T(8,128)}, u32[]{:S(2)}) copy-start(f32[64,8,24]{0,2,1:T(8,128)} %copy.77) | copy-start | bytes 147460
  258.0 9.5 %copy-start.8 = (f32[64,8,16]{2,0,1:T(8,128)S(1)}, f32[64,8,16]{2,0,1:T(8,128)}, u32[]{:S(2)}) copy-start(f32[64,8,16]{2,0,1:T(8,128)} %get-tuple-element.44) | copy-start | bytes 98308
  258.0 9.5 %copy-start.9 = (f32[64,8,16]{2,0,1:T(8,128)S(1)}, f32[64,8,16]{2,0,1:T(8,128)}, u32[]{:S(2)}) copy-start(f32[64,8,16]{2,0,1:T(8,128)} %get-tuple-element.49) | copy-start | bytes 98308
  258.0 9.5 %copy-start.10 = (f32[64,8,16]{2,0,1:T(8,128)S(1)}, f32[64,8,16]{2,0,1:T(8,128)}, u32[]{:S(2)}) copy-start(f32[64,8,16]{2,0,1:T(8,128)} %get-tuple-element.50) | copy-start | bytes 98308
  275.4 7.8 %copy-start.1 = (bf16[64,8,24,16]{3,0,2,1:T(8,128)(2,1)S(1)}, bf16[64,8,24,16]{3,0,2,1:T(8,128)(2,1)}, u32[]{:S(2)}) copy-start(bf16[64,8,24,16]{3,0,2,1:T(8,128)(2,1)} %get-tuple-element.11) | copy-start | bytes 1179652
  275.4 7.8 %copy-start.2 = (bf16[64,8,24,16]{3,0,2,1:T(8,128)(2,1)S(1)}, bf16[64,8,24,16]{3,0,2,1:T(8,128)(2,1)}, u32[]{:S(2)}) copy-start(bf16[64,8,24,16]{3,0,2,1:T(8,128)(2,1)} %get-tuple-element.12) | copy-start | bytes 1179652
  296.1 2.1 copy-start.7
  306.6 5.5 %copy-start.3 = (f32[2,32,8,1536]{3,2,0,1:T(8,128)S(1)}, f32[2,32,8,1536]{3,2,0,1:T(8,128)}, u32[]{:S(2)}) copy-start(f32[2,32,8,1536]{3,2,0,1:T(8,128)} %copy.70) | copy-start | bytes 9437188
Sparse Core Ops, SparseCore 0:
  9.6 79.6 all-gather.4
  91.5 46.2 all-gather.6
  140.0 79.5 all-gather.8
  221.7 46.2 all-gather.10
where the time goes:
time: 330 us; the launch traced here: 325 us
  waiting for transfers between devices  139 us (42%)
  other arithmetic  58.9 us (18%)
  matrix products  55.3 us (17%)
  local copies, waits for them, and re-layouts  43.2 us (13%)
  starting transfers between devices  15.1 us (5%)
  between operations  13.8 us (4%)
    all_gather x2, waiting for transfers between devices, project_qkv(): lax.all_gather(weight, 'fsdp', axis=1, tiled=True)  73.2 us
    all_to_all x1, waiting for transfers between devices, on_device(): lax.all_to_all(tiles.reshape(count, slots, width), 'fsdp', split_axis=0,...  27.7 us
    all_to_all x1, waiting for transfers between devices, on_device(): lax.all_to_all(hidden, 'fsdp', split_axis=1, concat_axis=0, tiled=True)  25.1 us
    dot_general x2, matrix products, multiply(): return jnp.dot(normed, piece, preferred_element_type=jnp.float32)  21.8 us
    another operation x4, other arithmetic  16.8 us
    dot_general x2, matrix products, attend(): jnp.einsum(score_form, query, key, preferred_element_type=jnp.float32)  15.3 us
    reduce_sum x4, other arithmetic, head_norm(): scale = lax.rsqrt(jnp.mean(values * values, axis=-1, keepdims=True) + EPS)  13.1 us
    convert_element_type x3, local copies, waits for them, and re-layouts, attend(): (mixed / total[..., None]).reshape(qkv.shape[:-1] + (width,))  12.4 us
  transfers between devices with their start and end apart: 6, of which 5 were waited for; matrix products, arithmetic and copies ran while one was open for 46% of the time, Pallas kernels for 0%

commit v1 on v0

--- a/solution.py
+++ b/solution.py
@@ -1,3 +1,4 @@
+import functools
 import jax
 import jax.numpy as jnp
 from jax import lax
@@ -5,6 +6,21 @@
 
 HEADS = 24
 EPS = 1e-06
+
+
+def shape_ports_on(array_in, comm_axis):
+    return jnp.concatenate(
+        jax.lax.all_to_all(
+            jnp.stack(tuple((array_in for _ in range(jax.lax.axis_size(comm_axis))))),
+            comm_axis,
+            0,
+            0,
+        ),
+        axis=1,
+    )
+
+
+detail_the_edge = functools.partial(shape_ports_on, comm_axis="fsdp")
 
 
 def rms_norm(grid, gain):
@@ -78,9 +94,7 @@
     def multiply(piece, start):
         return jnp.dot(normed, piece, preferred_element_type=jnp.float32)
 
-    return multiply(lax.all_gather(weight, "fsdp", axis=1, tiled=True), jnp.int32(0)).astype(
-        jnp.bfloat16
-    )
+    return multiply(detail_the_edge(weight), jnp.int32(0)).astype(jnp.bfloat16)
 
 
 def project_out(mixed, weight):

time: 330 us -> 618 us (1.87)
  the two profiles are of different devices: /device:TPU:1 before, /device:TPU:0 now
where the time goes in v1:
time: 618 us; the launch traced here: 612 us
  waiting for transfers between devices  363 us (59%)
  other arithmetic  59.3 us (10%)
  blocking collectives  57.9 us (9%)
  matrix products  54.5 us (9%)
  local copies, waits for them, and re-layouts  52.8 us (9%)
  between operations  14.2 us (2%)
  starting transfers between devices  10.4 us (2%)
    all_to_all x2, waiting for transfers between devices, shape_ports_on(): jax.lax.all_to_all(jnp.stack(tuple((array_in for _ in range(jax.lax.axis_...  361 us
    all_to_all x1, blocking collectives, on_device(): lax.all_to_all(tiles.reshape(count, slots, width), 'fsdp', split_axis=0,...  31.4 us
    all_to_all x1, blocking collectives, on_device(): lax.all_to_all(hidden, 'fsdp', split_axis=1, concat_axis=0, tiled=True)  26.5 us
    dot_general x2, matrix products, multiply(): return jnp.dot(normed, piece, preferred_element_type=jnp.float32)  22.3 us
    another operation x4, other arithmetic  16.7 us
    dot_general x2, matrix products, attend(): jnp.einsum(score_form, query, key, preferred_element_type=jnp.float32)  15.3 us
    another operation x2, local copies, waits for them, and re-layouts, shape_ports_on(): jnp.stack(tuple((array_in for _ in range(jax.lax.axis_size(comm_axis)))))  13.5 us
    reduce_sum x4, other arithmetic, head_norm(): scale = lax.rsqrt(jnp.mean(values * values, axis=-1, keepdims=True) + EPS)  12.7 us
  transfers between devices with their start and end apart: 4, of which 2 were waited for; matrix products, arithmetic and copies ran while one was open for 23% of the time, Pallas kernels for 0%

profile of v1, /device:TPU:0, one launch (start us, length us, event | category | flops | bytes accessed | tf_op | source)
XLA Modules:
  0.0 611.9 jit_solution(7815009994998030511)
XLA Ops:
  6.5 31.4 %all_to_all.24 = bf16[32,16,1536]{2,1,0:T(8,128)(2,1)S(1)} all-to-all(bf16[32,16,1536]{2,1,0:T(8,128)(2,1)} %bitcast.79), channel_id=1, replica_groups=mesh['fsdp'=32,'slide'=4] {'fsdp'}, dimensions={0} | all-to-all | bytes 3145728 | tf_op jit(solution)/shard_map/all_to_all | solution.py:118
  37.9 6.7 %stack.4 = bf16[32,1536,144]{1,2,0:T(8,128)(2,1)} broadcast(bf16[1536,144]{0,1:T(8,128)(2,1)S(1)} %copy-done.12), dimensions={1,2} | broadcast | bytes 14598144 | tf_op jit(solution)/shard_map/stack | solution.py:14
  44.7 5.2 all-to-all-start.1
  51.6 3.4 scatter_custom_fusion
  55.4 181.9 %all-to-all-done.1 = bf16[32,1536,144]{1,2,0:T(8,128)(2,1)} async-done(((bf16[32,1536,144]{1,2,0:T(8,128)(2,1)}), bf16[32,1536,144]{1,2,0:T(8,128)(2,1)}, u32[]{:S(2)}, u32[]{:S(2)}) %all-to-all-start.1) | async-done | bytes 14155808 | tf_op jit(solution)/shard_map/all_to_all | solution.py:13
  237.3 11.1 %convolution_convert_fusion.1 = bf16[512,4608]{1,0:T(8,128)(2,1)S(1)} fusion(bf16[1536,4608]{0,1:T(8,128)(2,1)} %bitcast.4, bf16[512,1536]{1,0:T(8,128)(2,1)S(1)} %scatter_custom_fusion, f32[1536]{0:T(1024)S(1)} %get-tuple-element.6, f32[512]{0:T(512)S(1)} %add_rsqrt_fusion.5), kind=kOutput, calls=%fused_computation.7 | convolution fusion | flops 7253262336 | bytes 20455424 | tf_op jit(solution)/shard_map/dot_general | solution.py:95
  269.7 3.5 fusion.39
  275.2 5.0 fusion.45
  281.8 26.5 %all_to_all.25 = bf16[2,256,1536]{2,0,1:T(2,128)(2,1)} all-to-all(bf16[2,256,1536]{2,0,1:T(2,128)(2,1)S(1)} %copy.68), channel_id=1, replica_groups=mesh['fsdp'=32,'slide'=4] {'fsdp'}, dimensions={1} | all-to-all | bytes 3145728 | tf_op jit(solution)/shard_map/all_to_all | solution.py:138
  308.3 6.7 %stack.5 = bf16[32,1536,144]{1,2,0:T(8,128)(2,1)} broadcast(bf16[1536,144]{0,1:T(8,128)(2,1)S(1)} %copy-done.13), dimensions={1,2} | broadcast | bytes 14598144 | tf_op jit(solution)/shard_map/stack | solution.py:14
  315.0 5.1 all-to-all-start.3
  328.0 179.6 %all-to-all-done.3 = bf16[32,1536,144]{1,2,0:T(8,128)(2,1)} async-done(((bf16[32,1536,144]{1,2,0:T(8,128)(2,1)}), bf16[32,1536,144]{1,2,0:T(8,128)(2,1)}, u32[]{:S(2)}, u32[]{:S(2)}) %all-to-all-start.3) | async-done | bytes 14155808 | tf_op jit(solution)/shard_map/all_to_all | solution.py:13
  507.6 11.2 %fusion.3 = bf16[64,8,4608]{2,1,0:T(8,128)(2,1)S(1)} fusion(bf16[512,1536]{1,0:T(8,128)(2,1)} %bitcast.84, bf16[1536,4608]{0,1:T(8,128)(2,1)} %bitcast.19), kind=kOutput, calls=%fused_computation.8 | convolution fusion | flops 7250116608 | bytes 20447232 | tf_op jit(solution)/shard_map/dot_general | solution.py:95
  521.9 5.5 reshape.279
  527.3 5.2 multiply_reduce_fusion
  534.3 3.5 reshape.278
  537.8 4.6 multiply_reduce_fusion.1
  545.8 9.3 %fusion.7 = (f32[64,8,24,64]{3,0,2,1:T(8,128)S(1)}, f32[64,8,24,64]{3,0,2,1:T(8,128)S(1)}) fusion(f32[64,8,24,64]{3,2,1,0:T(8,128)} %reshape.279, f32[64]{0:T(128)S(1)} %get-tuple-element.37, f32[64,8,24]{0,2,1:T(8,128)S(1)} %add_rsqrt_fusion, f32[64]{0:T(128)S(1)} %get-tuple-element.40, f32[64,8,24]{0,2,1:T(8,128)S(1)} %add_rsqrt_fusion.1, ...), kind=kLoop, calls=%fused_computation.13 | loop fusion | flops 3145728 | bytes 12681728 | tf_op jit(solution)/shard_map/mul | solution.py:34
  555.1 7.9 %subtract_convert_fusion.3 = (bf16[64,8,24,16]{3,0,2,1:T(8,128)(2,1)}, bf16[64,8,24,16]{3,0,2,1:T(8,128)(2,1)}, bf16[64,8,24,16]{3,0,2,1:T(8,128)(2,1)}, bf16[64,8,24,16]{3,0,2,1:T(8,128)(2,1)}) fusion(f32[64,8,24,64]{3,0,2,1:T(8,128)S(1)} %get-tuple-element.58, f32[64,8,16]{2,0,1:T(8,128)S(1)} %copy-done.8, f32[64,8,16]{2,0,1:T(8,128)S(1)} %get-tuple-element.43, ...), kind=kLoop, calls=%fused_computation.26 | loop fusion | flops 3145728 | bytes 4849664 | tf_op jit(solution)/shard_map/convert.13
  563.0 7.8 %subtract_convert_fusion.1 = (bf16[64,8,24,16]{3,0,2,1:T(8,128)(2,1)}, bf16[64,8,24,16]{3,0,2,1:T(8,128)(2,1)}, bf16[64,8,24,16]{3,0,2,1:T(8,128)(2,1)}, bf16[64,8,24,16]{3,0,2,1:T(8,128)(2,1)}) fusion(f32[64,8,24,64]{3,0,2,1:T(8,128)S(1)} %get-tuple-element.57, f32[64,8,16]{2,0,1:T(8,128)S(1)} %copy-done.8, f32[64,8,16]{2,0,1:T(8,128)S(1)} %get-tuple-element.43, ...), kind=kLoop, calls=%fused_computation.21 | loop fusion | flops 3145728 | bytes 4849664 | tf_op jit(solution)/shard_map/convert.9
  570.8 13.0 %fusion.13 = (f32[8,24,64]{2,1,0:T(8,128)S(1)}, f32[8,24,64,64]{2,3,1,0:T(8,128)S(1)}) fusion(pred[8,64,64]{1,2,0:T(8,128)(4,1)S(1)} %broadcast_or_fusion.1, bf16[64,8,24,16]{3,0,2,1:T(8,128)(2,1)} %get-tuple-element.15, bf16[64,8,24,16]{3,0,2,1:T(8,128)(2,1)} %get-tuple-element.16, bf16[64,8,24,16]{3,0,2,1:T(8,128)(2,1)} %get-tuple-element.8, ...), kind=kOutput, calls=%fused_computation.32 | convolution fusion | flops 115593216 | bytes 6373376 | tf_op jit(solution)/shard_map/lbhd,mbhd->bhlm/dot_general | solution.py:74
  587.9 3.8 copy.79
  591.7 4.5 convert_element_type.216
  598.3 6.5 %fusion.46 = bf16[64,8,1536]{2,1,0:T(8,128)(2,1)} fusion(f32[512,1536]{1,0:T(8,128)} %bitcast.78, bf16[512,1536]{1,0:T(8,128)(2,1)S(1)} %convert_element_type.216, bf16[1536,1536]{0,1:T(8,128)(2,1)} %all-gather.5.cloned.1.call-done), kind=kOutput, calls=%fused_computation.75 | convolution fusion | flops 2417491968 | bytes 11010048 | tf_op jit(solution)/shard_map/dot_general | solution.py:103
  (98 shorter events, 49.0 us)
Async XLA Ops:
  6.5 31.4 %copy-start.12 = (bf16[1536,144]{0,1:T(8,128)(2,1)S(1)}, bf16[1536,144]{0,1:T(8,128)(2,1)}, u32[]{:S(2)}) copy-start(bf16[1536,144]{0,1:T(8,128)(2,1)} %param.14) | copy-start | bytes 1327108
  44.7 6.0 copy-start.15
  44.7 6.4 %copy-start.16 = (s32[64,256]{1,0:T(8,128)S(1)}, s32[64,256]{1,0:T(8,128)}, u32[]{:S(2)}) copy-start(s32[64,256]{1,0:T(8,128)} %param.11) | copy-start | bytes 196612
  44.7 6.4 %copy-start.18 = (f32[2,2,64]{2,1,0:T(2,128)S(1)}, f32[2,2,64]{2,1,0:T(2,128)}, u32[]{:S(2)}) copy-start(f32[2,2,64]{2,1,0:T(2,128)} %param.13) | copy-start | bytes 3076
  44.7 6.5 %copy-start.17 = (f32[2,1536]{1,0:T(2,128)S(1)}, f32[2,1536]{1,0:T(2,128)}, u32[]{:S(2)}) copy-start(f32[2,1536]{1,0:T(2,128)} %param.12) | copy-start | bytes 36868
  44.7 192.6 %all-to-all-start.1 = ((bf16[32,1536,144]{1,2,0:T(8,128)(2,1)}), bf16[32,1536,144]{1,2,0:T(8,128)(2,1)}, u32[]{:S(2)}, u32[]{:S(2)}) async-start(bf16[32,1536,144]{1,2,0:T(8,128)(2,1)} %stack.4), calls=%async_computation.1 | async-start | bytes 28311552 | tf_op jit(solution)/shard_map/all_to_all | solution.py:13
  49.9 225.2 %all-gather.3.cloned.1.call-start = ((), (), s32[]{:S(2)}) async-start(), calls=%async_computation.4 | async-start | bytes 4866048 | tf_op jit(solution)/shard_map/all_gather | solution.py:105
  55.0 193.4 %copy-start.4 = (bf16[512,1536]{1,0:T(8,128)(2,1)}, bf16[512,1536]{1,0:T(8,128)(2,1)S(1)}, u32[]{:S(2)}) copy-start(bf16[512,1536]{1,0:T(8,128)(2,1)S(1)} %scatter_custom_fusion) | copy-start | bytes 4718596
  258.9 2.9 copy-start
  266.5 3.1 copy-start.11
  273.1 2.0 copy-start.5
  280.2 28.1 %copy-start.13 = (bf16[1536,144]{0,1:T(8,128)(2,1)S(1)}, bf16[1536,144]{0,1:T(8,128)(2,1)}, u32[]{:S(2)}) copy-start(bf16[1536,144]{0,1:T(8,128)(2,1)} %param.16) | copy-start | bytes 1327108
  315.0 192.5 %all-to-all-start.3 = ((bf16[32,1536,144]{1,2,0:T(8,128)(2,1)}), bf16[32,1536,144]{1,2,0:T(8,128)(2,1)}, u32[]{:S(2)}, u32[]{:S(2)}) async-start(bf16[32,1536,144]{1,2,0:T(8,128)(2,1)} %stack.5), calls=%async_computation.3 | async-start | bytes 28311552 | tf_op jit(solution)/shard_map/all_to_all | solution.py:13
  320.1 278.2 %all-gather.5.cloned.1.call-start = ((), (), s32[]{:S(2)}) async-start(), calls=%async_computation.5 | async-start | bytes 4866048 | tf_op jit(solution)/shard_map/all_gather | solution.py:105
  537.8 4.8 copy-start.6
  542.4 3.4 copy-start.14
  545.8 9.3 %copy-start.8 = (f32[64,8,16]{2,0,1:T(8,128)S(1)}, f32[64,8,16]{2,0,1:T(8,128)}, u32[]{:S(2)}) copy-start(f32[64,8,16]{2,0,1:T(8,128)} %get-tuple-element.44) | copy-start | bytes 98308
  545.8 9.3 %copy-start.9 = (f32[64,8,16]{2,0,1:T(8,128)S(1)}, f32[64,8,16]{2,0,1:T(8,128)}, u32[]{:S(2)}) copy-start(f32[64,8,16]{2,0,1:T(8,128)} %get-tuple-element.49) | copy-start | bytes 98308
  545.8 9.3 %copy-start.10 = (f32[64,8,16]{2,0,1:T(8,128)S(1)}, f32[64,8,16]{2,0,1:T(8,128)}, u32[]{:S(2)}) copy-start(f32[64,8,16]{2,0,1:T(8,128)} %get-tuple-element.50) | copy-start | bytes 98308
  563.0 7.8 %copy-start.2 = (bf16[64,8,24,16]{3,0,2,1:T(8,128)(2,1)S(1)}, bf16[64,8,24,16]{3,0,2,1:T(8,128)(2,1)}, u32[]{:S(2)}) copy-start(bf16[64,8,24,16]{3,0,2,1:T(8,128)(2,1)} %get-tuple-element.11) | copy-start | bytes 1179652
  563.0 7.8 %copy-start.3 = (bf16[64,8,24,16]{3,0,2,1:T(8,128)(2,1)S(1)}, bf16[64,8,24,16]{3,0,2,1:T(8,128)(2,1)}, u32[]{:S(2)}) copy-start(bf16[64,8,24,16]{3,0,2,1:T(8,128)(2,1)} %get-tuple-element.12) | copy-start | bytes 1179652
  583.7 2.2 copy-start.7
  591.7 4.5 copy-start.1
Sparse Core Ops, SparseCore 0:
  53.0 167.7 all-gather.2
  323.2 167.7 all-gather.4
